TPU v7x, 32 devices: a whole 2x2x4 slice. The times are simulated.
32 devices in a mesh: grp: 2 (over x), tm: 16 (over z, y, core).
Axes of the slice: x: 2, y: 2, z: 4, core: 2. Of those that a mesh axis runs over, the one named last changes fastest.
Arguments:
- waveform: float32 [262144], P(('grp', 'tm')), parts along dimension 0, may hold values from -8 to 8
- enc_weight: float32 [16, 256], replicated, may hold values from -1.5 to 1.5
- intra_qkv: bfloat16 [256, 768], replicated, may hold values from -3 to 3
- intra_out: bfloat16 [256, 256], replicated, may hold values from -0.375 to 0.375
- intra_up: bfloat16 [256, 1024], replicated, may hold values from -0.375 to 0.375
- intra_down: bfloat16 [1024, 256], replicated, may hold values from -0.1875 to 0.1875
- inter_qkv: bfloat16 [256, 768], replicated, may hold values from -3 to 3
- inter_out: bfloat16 [256, 256], replicated, may hold values from -0.375 to 0.375
- inter_up: bfloat16 [256, 1024], replicated, may hold values from -0.375 to 0.375
- inter_down: bfloat16 [1024, 256], replicated, may hold values from -0.1875 to 0.1875
- mask_weight: bfloat16 [256, 512], replicated, may hold values from -0.375 to 0.375
Outputs:
- separated: bfloat16 [2, 32768, 256], P(None, ('grp', 'tm')), parts along dimension 1
There are 2 independent parts, one for each index of `grp`. A program takes and returns all parts, laid end to end along the dimension named above; an argument that names none is the same for every part. Nothing has to cross between parts.
All inputs are finite; a program needn't handle non-finite values.
Results may differ from a plain program's by a relative error of at most 0.011.
Values may be sent and summed in bfloat16 or wider, within the bound.
No kernel may reach another device: no remote copies, remote signals or barrier semaphores. Data moves between devices by JAX's collectives and lax.ppermute only.
A program may use at most 192 MiB of HBM per device.

v0:
```python
import jax
import jax.numpy as jnp
from jax import lax
from jax.sharding import PartitionSpec as P

HEADS = 8
HEAD = 32
HOP = 8
HALF = 128


def shifted(value, axis, steps):
    count = lax.axis_size(axis)
    leading, last = (max(0, -steps), min(count, count - steps))
    return lax.ppermute(value, axis, [(source, source + steps) for source in range(leading, last)])


def rounded(values):
    return lax.optimization_barrier(values.astype(jnp.bfloat16))


def layer_norm(values):
    values = values.astype(jnp.float32)
    centred = values - jnp.mean(values, axis=-1, keepdims=True)
    spread = jnp.mean(centred * centred, axis=-1, keepdims=True)
    return centred * lax.rsqrt(spread + 1e-05)


def project(values, weight):
    flattened = values.reshape(-1, values.shape[-1])
    result = jnp.dot(flattened, weight, preferred_element_type=jnp.float32)
    return result.reshape(values.shape[:-1] + (weight.shape[1],))


def attend(queries, key_rows, value_rows, seq_first):
    full_shape = queries.shape
    split_shape = full_shape[:-1] + (HEADS, HEAD)
    query_heads = queries.reshape(split_shape)
    key_heads = key_rows.reshape(split_shape)
    value_heads = value_rows.reshape(split_shape)
    if seq_first:
        score_form = "lbhe,kbhe->bhlk"
        weigh_form = "bhlk,kbhe->lbhe"
    else:
        score_form = "blhe,bkhe->bhlk"
        weigh_form = "bhlk,bkhe->blhe"
    scores = jnp.einsum(
        score_form, query_heads, key_heads, preferred_element_type=jnp.float32
    ) * HEAD ** (-0.5)
    probs = jax.nn.softmax(scores, axis=-1).astype(jnp.bfloat16)
    mixture = jnp.einsum(weigh_form, probs, value_heads, preferred_element_type=jnp.float32)
    return mixture.astype(jnp.bfloat16).reshape(full_shape)


def transformer_layer(tokens, weights, seq_first):
    qkv_weight, out_weight, up_weight, down_weight = weights
    model_width = tokens.shape[-1]
    normed = layer_norm(tokens).astype(jnp.bfloat16)
    triple = project(normed, qkv_weight).astype(jnp.bfloat16)
    attended = attend(
        triple[..., :model_width],
        triple[..., model_width : 2 * model_width],
        triple[..., 2 * model_width :],
        seq_first,
    )
    after_attention = rounded(tokens.astype(jnp.float32) + project(attended, out_weight))
    normed_again = layer_norm(after_attention).astype(jnp.bfloat16)
    hidden = jax.nn.relu(project(normed_again, up_weight)).astype(jnp.bfloat16)
    return (after_attention.astype(jnp.float32) + project(hidden, down_weight)).astype(jnp.bfloat16)


def encode(framed, enc_weight):
    return rounded(
        jax.nn.relu(
            jnp.dot(
                framed,
                enc_weight,
                precision=lax.Precision.HIGHEST,
                preferred_element_type=jnp.float32,
            )
        )
    )


def local(
    waveform,
    enc_weight,
    intra_qkv,
    intra_out,
    intra_up,
    intra_down,
    inter_qkv,
    inter_out,
    inter_up,
    inter_down,
    mask_weight,
):
    model_width = enc_weight.shape[1]
    frames_here = waveform.shape[0] // HOP
    blocks = waveform.reshape(frames_here, HOP)
    first_block = shifted(blocks[:1], "tm", -1)
    following = jnp.concatenate([blocks[1:], first_block], axis=0)
    framed = jnp.concatenate([blocks, following], axis=1)
    encoded = encode(framed, enc_weight)
    frame_edge = shifted(encoded[:HALF], "tm", -1)
    padded = jnp.concatenate([encoded, frame_edge], axis=0)
    segment_total = frames_here // HALF
    stacked = padded.reshape(segment_total + 1, HALF, model_width)
    segmented = jnp.concatenate([stacked[:-1], stacked[1:]], axis=1)
    intra_weights = (intra_qkv, intra_out, intra_up, intra_down)
    inter_weights = (inter_qkv, inter_out, inter_up, inter_down)
    within = transformer_layer(segmented, intra_weights, False)
    within = within.reshape(segment_total, 2, HALF, model_width)
    pieces = lax.all_to_all(within, "tm", split_axis=2, concat_axis=0, tiled=True)
    row_total, item_count, spot_count, feature_count = pieces.shape
    flattened = pieces.reshape(row_total, item_count * spot_count, feature_count)
    result = transformer_layer(flattened, inter_weights, True)
    across = result.reshape(row_total, item_count, spot_count, feature_count)
    returned = lax.all_to_all(across, "tm", split_axis=0, concat_axis=2, tiled=True)
    tail_half = shifted(returned[-1:, 1], "tm", 1)
    lagged = jnp.concatenate([tail_half, returned[:-1, 1]], axis=0)
    combined = rounded(returned[:, 0].astype(jnp.float32) + lagged.astype(jnp.float32))
    combined = combined.reshape(frames_here, model_width)
    activated = combined.astype(jnp.float32)
    activated = jnp.where(activated > 0, activated, 0.25 * activated).astype(jnp.bfloat16)
    mask_values = jax.nn.relu(jnp.dot(activated, mask_weight, preferred_element_type=jnp.float32))
    mask_values = mask_values.reshape(frames_here, 2, model_width)
    separated = (mask_values * encoded.astype(jnp.float32)[:, None, :]).astype(jnp.bfloat16)
    return jnp.transpose(separated, (1, 0, 2))


def solution(mesh):
    return jax.shard_map(
        local,
        mesh=mesh,
        in_specs=(P(("grp", "tm")), P(), P(), P(), P(), P(), P(), P(), P(), P(), P()),
        out_specs=P(None, ("grp", "tm"), None),
        check_vma=False,
    )
```

profile of v0, /device:TPU:0, one launch (start us, length us, event | category | flops | bytes accessed | tf_op | source)
XLA Modules:
  0.0 149.3 jit_solution(12146366738658521298)
XLA Ops:
  0.8 1.3 collective-permute-start
  2.1 0.8 slice.60
  2.9 1.1 reshape.185
  4.7 1.1 fusion.41
  5.8 1.4 collective-permute-start.1
  7.3 3.8 %collective-permute-done.1 = bf16[128,256]{1,0:T(8,128)(2,1)S(1)} collective-permute-done((bf16[128,256]{1,0:T(8,128)(2,1)S(1)}, bf16[128,256]{1,0:T(8,128)(2,1)S(1)}, u32[]{:S(2)}, u32[]{:S(2)}) %collective-permute-start.1) | collective-permute-done | bytes 65568 | tf_op jit(solution)/shard_map/ppermute | solution.py:15
  11.0 1.1 fusion.91
  13.1 1.5 %convolution_convert_fusion.1 = bf16[8,256,768]{2,1,0:T(8,128)(2,1)S(1)} fusion(f32[8,256]{1,0:T(8,128)S(1)} %add_rsqrt_fusion.3, f32[8,256]{1,0:T(8,128)S(1)} %broadcast_multiply_fusion.3, bf16[256,768]{1,0:T(8,128)(2,1)S(1)} %copy-done.10, bf16[8,128,256]{2,1,0:T(8,128)(2,1)S(1)} %bitcast.108, bf16[8,128,256]{2,1,0:T(8,128)(2,1)S(1)} %bitcast.103), kind=kOutput, calls=%fused_computation.40 | convolution fusion | flops 810549248 | bytes 4603904 | tf_op jit(solution)/shard_map/dot_general | solution.py:31
  14.7 1.7 %fusion.90 = (bf16[8,256,256]{2,1,0:T(8,128)(2,1)}, bf16[8,256,256]{2,1,0:T(8,128)(2,1)}, bf16[8,256,256]{2,1,0:T(8,128)(2,1)S(1)}) fusion(bf16[8,256,768]{2,1,0:T(8,128)(2,1)S(1)} %convolution_convert_fusion.1), kind=kLoop, calls=%fused_computation.113 | loop fusion | bytes 6291456 | tf_op jit(solution)/shard_map/slice | solution.py:62
  16.4 2.3 %copy.43 = bf16[8,256,256]{1,2,0:T(8,128)(2,1)} copy(bf16[8,256,256]{2,1,0:T(8,128)(2,1)} %get-tuple-element.8) | data formatting | bytes 2097152 | tf_op jit(solution)/shard_map/slice | solution.py:62
  18.7 2.3 %copy.42 = bf16[8,256,256]{1,2,0:T(8,128)(2,1)} copy(bf16[8,256,256]{2,1,0:T(8,128)(2,1)} %get-tuple-element.9) | data formatting | bytes 2097152 | tf_op jit(solution)/shard_map/slice | solution.py:61
  21.0 1.3 copy.41
  22.3 10.3 %fusion.92 = (f32[8,8,256]{2,1,0:T(8,128)S(1)}, f32[8,8,256,256]{2,3,1,0:T(8,128)}) fusion(bf16[8,256,8,32]{1,3,2,0:T(8,128)(2,1)} %bitcast.117, bf16[8,256,8,32]{1,3,2,0:T(8,128)(2,1)} %bitcast.115), kind=kOutput, calls=%fused_computation.115 | convolution fusion | flops 281018624 | bytes 18939904 | tf_op jit(solution)/shard_map/sub | solution.py:50
  32.6 7.4 %fusion.39 = bf16[8,8,32,256]{3,2,1,0:T(8,128)(2,1)S(1)} fusion(bf16[8,256,8,32]{1,3,2,0:T(8,128)(2,1)S(1)} %bitcast.118, f32[8,8,256,256]{2,3,1,0:T(8,128)} %get-tuple-element.14, f32[8,8,256]{2,1,0:T(8,128)S(1)} %get-tuple-element.13), kind=kOutput, calls=%fused_computation.58 | convolution fusion | flops 277348352 | bytes 18939904 | tf_op jit(solution)/shard_map/bhlk,bkhe->blhe/dot_general | solution.py:51
  41.5 2.5 %fusion.35 = bf16[8,256,256]{2,1,0:T(8,128)(2,1)S(1)} fusion(bf16[8,256,256]{2,1,0:T(8,128)(2,1)S(1)} %fusion.34, f32[8,256]{1,0:T(8,128)S(1)} %add_rsqrt_fusion.2, f32[8,256]{1,0:T(8,128)S(1)} %broadcast_multiply_fusion.2, bf16[1024,256]{1,0:T(8,128)(2,1)S(1)} %copy-done, bf16[256,1024]{1,0:T(8,128)(2,1)S(1)} %copy-done.8), kind=kOutput, calls=%fused_computation.48 | convolution fusion | flops 2155347968 | bytes 3162112 | tf_op jit(solution)/shard_map/dot_general | solution.py:31
  44.0 1.1 copy.46
  45.1 33.6 %all_to_all.27 = bf16[8,2,128,256]{3,1,0,2:T(2,128)(2,1)S(1)} all-to-all(bf16[8,2,128,256]{3,1,0,2:T(2,128)(2,1)S(1)} %copy.46), channel_id=1, replica_groups=mesh['grp'=2,'tm'=16] {'tm'}, dimensions={2} | all-to-all | bytes 2097152 | tf_op jit(solution)/shard_map/all_to_all | solution.py:114
  78.7 1.1 bitcast_convert_fusion
  81.9 1.5 %convolution_convert_fusion = bf16[128,16,768]{2,0,1:T(8,128)(2,1)S(1)} fusion(f32[128,16,256]{2,0,1:T(8,128)S(1)} %bitcast.98, f32[128,16]{0,1:T(8,128)S(1)} %rsqrt.38, f32[128,16]{0,1:T(8,128)S(1)} %div.49, bf16[256,768]{1,0:T(8,128)(2,1)S(1)} %copy-done.4), kind=kOutput, calls=%fused_computation.39 | convolution fusion | flops 808452096 | bytes 5652480 | tf_op jit(solution)/shard_map/dot_general | solution.py:31
  83.5 1.7 %fusion.89 = (bf16[128,16,256]{2,0,1:T(8,128)(2,1)}, bf16[128,16,256]{2,0,1:T(8,128)(2,1)}, bf16[128,16,256]{2,0,1:T(8,128)(2,1)S(1)}) fusion(bf16[128,16,768]{2,0,1:T(8,128)(2,1)S(1)} %convolution_convert_fusion), kind=kLoop, calls=%fused_computation.112 | loop fusion | bytes 6291456 | tf_op jit(solution)/shard_map/slice | solution.py:62
  85.2 2.3 %copy.50 = bf16[128,16,256]{0,2,1:T(8,128)(2,1)} copy(bf16[128,16,256]{2,0,1:T(8,128)(2,1)} %get-tuple-element.5) | data formatting | bytes 2097152 | tf_op jit(solution)/shard_map/slice | solution.py:62
  87.4 2.3 %copy.49 = bf16[128,16,256]{0,2,1:T(8,128)(2,1)} copy(bf16[128,16,256]{2,0,1:T(8,128)(2,1)} %get-tuple-element.6) | data formatting | bytes 2097152 | tf_op jit(solution)/shard_map/slice | solution.py:61
  89.8 1.3 copy.48
  91.1 8.1 %fusion.93 = (f32[16,8,128]{2,1,0:T(8,128)S(1)}, f32[16,8,128,128]{2,3,1,0:T(8,128)}) fusion(bf16[128,16,8,32]{0,3,2,1:T(8,128)(2,1)} %bitcast.119, bf16[128,16,8,32]{0,3,2,1:T(8,128)(2,1)} %bitcast.116), kind=kOutput, calls=%fused_computation.116 | convolution fusion | flops 140509312 | bytes 10551296 | tf_op jit(solution)/shard_map/sub | solution.py:50
  99.2 4.6 %fusion.40 = bf16[16,8,32,128]{3,2,1,0:T(8,128)(2,1)S(1)} fusion(bf16[128,16,8,32]{0,3,2,1:T(8,128)(2,1)S(1)} %bitcast.120, f32[16,8,128,128]{2,3,1,0:T(8,128)} %get-tuple-element.16, f32[16,8,128]{2,1,0:T(8,128)S(1)} %get-tuple-element.15), kind=kOutput, calls=%fused_computation.59 | convolution fusion | flops 138936320 | bytes 10551296 | tf_op jit(solution)/shard_map/bhlk,kbhe->lbhe/dot_general | solution.py:51
  105.3 3.5 %fusion.36 = bf16[128,16,256]{2,0,1:T(8,128)(2,1)S(1)} fusion(bf16[128,16,256]{2,0,1:T(8,128)(2,1)S(1)} %add_convert_fusion, f32[128,16]{0,1:T(8,128)S(1)} %add_rsqrt_fusion.1, f32[128,16]{0,1:T(8,128)S(1)} %broadcast_multiply_fusion.1, bf16[1024,256]{1,0:T(8,128)(2,1)S(1)} %copy-done.9, bf16[256,1024]{1,0:T(8,128)(2,1)} %param.19), kind=kOutput, calls=%fused_computation.49 | convolution fusion | flops 2155347968 | bytes 3162112 | tf_op jit(solution)/shard_map/dot_general | solution.py:31
  109.5 29.5 %all_to_all.28 = bf16[128,2,8,256]{3,2,1,0:T(8,128)(2,1)S(1)} all-to-all(bf16[128,2,8,256]{3,2,1,0:T(8,128)(2,1)S(1)} %copy.53), channel_id=1, replica_groups=mesh['grp'=2,'tm'=16] {'tm'}, dimensions={0} | all-to-all | bytes 2097152 | tf_op jit(solution)/shard_map/all_to_all | solution.py:119
  139.1 2.9 %collective-permute-start.2 = (bf16[1,128,256]{2,1,0:T(8,128)(2,1)S(1)}, bf16[1,128,256]{2,1,0:T(8,128)(2,1)S(1)}, u32[]{:S(2)}, u32[]{:S(2)}) collective-permute-start(bf16[1,128,256]{2,1,0:T(8,128)(2,1)S(1)} %slice_bitcast_fusion.2), channel_id=1, source_target_pairs={{0,1},{1,2},{2,3},{3,4},{4,5},{5,6},{6,7},{7,8},{8,9},{9,10},{10,1... | collective-permute-start | bytes 196616 | tf_op jit(solution)/shard_map/ppermute | solution.py:15
  142.0 0.8 collective-permute-done.2
  143.0 1.9 %convolution_maximum_fusion = f32[1024,512]{0,1:T(8,128)} fusion(bf16[256,512]{1,0:T(8,128)(2,1)S(1)} %copy-done.5, bf16[1024,256]{1,0:T(8,128)(2,1)S(1)} %bitcast.114), kind=kOutput, calls=%fused_computation.57 | convolution fusion | flops 270270464 | bytes 2883584 | tf_op jit(solution)/shard_map/dot_general | solution.py:126
  144.9 1.9 %copy.55 = f32[1024,2,256]{2,0,1:T(8,128)S(1)} copy(f32[1024,2,256]{0,2,1:T(8,128)} %bitcast.105) | data formatting | bytes 4194304 | tf_op jit(solution)/shard_map/reshape | solution.py:127
  146.8 2.5 %fusion.42 = bf16[2,1024,256]{2,1,0:T(8,128)(2,1)} fusion(f32[1024,2,256]{2,0,1:T(8,128)S(1)} %copy.55, f32[1024,256]{1,0:T(8,128)} %get-tuple-element.11), kind=kLoop, calls=%fused_computation.62 | loop fusion | flops 1048576 | bytes 4194304 | tf_op jit(solution)/shard_map/transpose | solution.py:129
  (57 shorter events, 8.4 us)
Async XLA Ops:
  0.0 41.5 %copy-start = (bf16[1024,256]{1,0:T(8,128)(2,1)S(1)}, bf16[1024,256]{1,0:T(8,128)(2,1)}, u32[]{:S(2)}) copy-start(bf16[1024,256]{1,0:T(8,128)(2,1)} %param.16) | copy-start | bytes 1572868
  0.0 4.7 %copy-start.7 = (f32[16,256]{1,0:T(8,128)S(1)}, f32[16,256]{1,0:T(8,128)}, u32[]{:S(2)}) copy-start(f32[16,256]{1,0:T(8,128)} %param.12) | copy-start | bytes 49156
  0.8 3.8 %collective-permute-start = (f32[1,8]{1,0:T(1,128)S(1)}, f32[1,8]{1,0:T(1,128)S(1)}, u32[]{:S(2)}, u32[]{:S(2)}) collective-permute-start(f32[1,8]{1,0:T(1,128)S(1)} %slice_bitcast_fusion.3), channel_id=1, source_target_pairs={{1,0},{2,1},{3,2},{4,3},{5,4},{6,5},{7,6},{8,7},{9,8},{10,9},{11,1... | collective-permute-start | bytes 104 | tf_op jit(solution)/shard_map/ppermute | solution.py:15
  5.8 7.3 %copy-start.10 = (bf16[256,768]{1,0:T(8,128)(2,1)S(1)}, bf16[256,768]{1,0:T(8,128)(2,1)}, u32[]{:S(2)}) copy-start(bf16[256,768]{1,0:T(8,128)(2,1)} %param.13) | copy-start | bytes 1179652
  5.8 5.2 %collective-permute-start.1 = (bf16[128,256]{1,0:T(8,128)(2,1)S(1)}, bf16[128,256]{1,0:T(8,128)(2,1)S(1)}, u32[]{:S(2)}, u32[]{:S(2)}) collective-permute-start(bf16[128,256]{1,0:T(8,128)(2,1)S(1)} %slice.77), channel_id=1, source_target_pairs={{1,0},{2,1},{3,2},{4,3},{5,4},{6,5},{7,6},{8,7},{9,8},{10,9},{11,1... | collective-permute-start | bytes 196616 | tf_op jit(solution)/shard_map/ppermute | solution.py:15
  22.3 10.3 %copy-start.2 = (bf16[8,256,256]{1,2,0:T(8,128)(2,1)S(1)}, bf16[8,256,256]{1,2,0:T(8,128)(2,1)}, u32[]{:S(2)}) copy-start(bf16[8,256,256]{1,2,0:T(8,128)(2,1)} %copy.41) | copy-start | bytes 3145732
  32.6 7.4 %copy-start.11 = (bf16[256,256]{1,0:T(8,128)(2,1)S(1)}, bf16[256,256]{1,0:T(8,128)(2,1)}, u32[]{:S(2)}) copy-start(bf16[256,256]{1,0:T(8,128)(2,1)} %param.14) | copy-start | bytes 393220
  40.0 1.5 %copy-start.8 = (bf16[256,1024]{1,0:T(8,128)(2,1)S(1)}, bf16[256,1024]{1,0:T(8,128)(2,1)}, u32[]{:S(2)}) copy-start(bf16[256,1024]{1,0:T(8,128)(2,1)} %param.15) | copy-start | bytes 1572868
  80.9 1.0 copy-start.4
  91.1 8.1 %copy-start.3 = (bf16[128,16,256]{0,2,1:T(8,128)(2,1)S(1)}, bf16[128,16,256]{0,2,1:T(8,128)(2,1)}, u32[]{:S(2)}) copy-start(bf16[128,16,256]{0,2,1:T(8,128)(2,1)} %copy.48) | copy-start | bytes 3145732
  99.2 4.6 %copy-start.6 = (bf16[256,256]{1,0:T(8,128)(2,1)S(1)}, bf16[256,256]{1,0:T(8,128)(2,1)}, u32[]{:S(2)}) copy-start(bf16[256,256]{1,0:T(8,128)(2,1)} %param.18) | copy-start | bytes 393220
  104.3 1.0 copy-start.9
  139.0 4.0 %copy-start.5 = (bf16[256,512]{1,0:T(8,128)(2,1)S(1)}, bf16[256,512]{1,0:T(8,128)(2,1)}, u32[]{:S(2)}) copy-start(bf16[256,512]{1,0:T(8,128)(2,1)} %param.21) | copy-start | bytes 786436
  139.1 3.8 %collective-permute-start.2 = (bf16[1,128,256]{2,1,0:T(8,128)(2,1)S(1)}, bf16[1,128,256]{2,1,0:T(8,128)(2,1)S(1)}, u32[]{:S(2)}, u32[]{:S(2)}) collective-permute-start(bf16[1,128,256]{2,1,0:T(8,128)(2,1)S(1)} %slice_bitcast_fusion.2), channel_id=1, source_target_pairs={{0,1},{1,2},{2,3},{3,4},{4,5},{5,6},{6,7},{7,8},{8,9},{9,10},{10,1... | collective-permute-start | bytes 196616 | tf_op jit(solution)/shard_map/ppermute | solution.py:15
  146.8 2.5 %copy-start.1 = (bf16[1024,256]{1,0:T(8,128)(2,1)S(1)}, bf16[1024,256]{1,0:T(8,128)(2,1)}, u32[]{:S(2)}) copy-start(bf16[1024,256]{1,0:T(8,128)(2,1)} %param.16) | copy-start | bytes 1572868
where the time goes:
time: 152 us; the launch traced here: 149 us
  blocking collectives  63.1 us (42%)
  matrix products  43.4 us (29%)
  local copies, waits for them, and re-layouts  23.3 us (15%)
  other arithmetic  8.87 us (6%)
  starting transfers between devices  5.58 us (4%)
  waiting for transfers between devices  4.61 us (3%)
    all_to_all x1, blocking collectives, local(): lax.all_to_all(within, 'tm', split_axis=2, concat_axis=0, tiled=True)  33.6 us
    all_to_all x1, blocking collectives, local(): lax.all_to_all(across, 'tm', split_axis=0, concat_axis=2, tiled=True)  29.5 us
    sub x2, matrix products, attend(): probs = jax.nn.softmax(scores, axis=-1).astype(jnp.bfloat16)  18.4 us
    dot_general x2, matrix products, attend(): jnp.einsum(weigh_form, probs, value_heads, preferred_element_type=jnp.flo...  12 us
    dot_general x6, matrix products, project(): result = jnp.dot(flattened, weight, preferred_element_type=jnp.float32)  10.1 us
    slice x4, local copies, waits for them, and re-layouts, transformer_layer(): triple[..., model_width:2 * model_width]  7.96 us
    ppermute x3, starting transfers between devices, shifted(): lax.ppermute(value, axis, [(source, source + steps) for source in range(l...  5.58 us
    slice x2, local copies, waits for them, and re-layouts, transformer_layer(): triple[..., :model_width]  4.62 us
  transfers between devices with their start and end apart: 3, of which 2 were waited for; matrix products, arithmetic and copies ran while one was open for 2% of the time, Pallas kernels for 0%

commit v1 on v0

--- a/solution.py
+++ b/solution.py
@@ -1,6 +1,10 @@
+import math
+
 import jax
 import jax.numpy as jnp
 from jax import lax
+from jax.experimental import pallas as pl
+from jax.experimental.pallas import tpu as pltpu
 from jax.sharding import PartitionSpec as P
 
 HEADS = 8
@@ -129,9 +133,349 @@
     return jnp.transpose(separated, (1, 0, 2))
 
 
+LANES = 128
+WITHIN_BATCH = 4
+SCORE_SCALE = math.log2(math.e) * HEAD ** (-0.5)
+
+
+def normalise(values):
+    mean = jnp.sum(values, axis=-1, keepdims=True) * (1.0 / values.shape[-1])
+    centred = values - mean
+    spread = jnp.sum(centred * centred, axis=-1, keepdims=True) * (1.0 / values.shape[-1])
+    return centred * lax.rsqrt(spread + 1e-05)
+
+
+def round_trip(values):
+    return values.astype(jnp.bfloat16).astype(jnp.float32)
+
+
+def matmul(left, right):
+    return jnp.dot(left, right, preferred_element_type=jnp.float32)
+
+
+def put(ref, rows, value, *lead):
+    for block in range(value.shape[1] // LANES):
+        ref[(*lead, block, rows, slice(None))] = value[:, block * LANES : (block + 1) * LANES]
+
+
+def get(ref, rows):
+    return jnp.concatenate([ref[block, rows, :] for block in range(ref.shape[0])], axis=1)
+
+
+def attend_rows(batch):
+    group = LANES // HEAD
+    work = []
+    for queries, keys, values in batch:
+        lane_head = lax.broadcasted_iota(jnp.int32, (queries.shape[0], LANES), 1) // HEAD
+        for half in range(queries.shape[1] // LANES):
+            columns = slice(half * LANES, (half + 1) * LANES)
+            part = queries[:, columns]
+            spread = [jnp.where(lane_head == head, part, 0.0) for head in range(group)]
+            spread = jnp.concatenate(spread, axis=0).astype(jnp.bfloat16)
+            work.append((matmul(spread, keys[columns, :]), values[:, columns]))
+    shares = []
+    for scores, part in work:
+        peak = jnp.max(scores, axis=-1, keepdims=True)
+        weights = jnp.exp2((scores - peak) * SCORE_SCALE)
+        total = jnp.sum(weights, axis=-1, keepdims=True)
+        shares.append((weights.astype(jnp.bfloat16), total, part))
+    mixed = [matmul(weights, part) * (1.0 / total) for weights, total, part in shares]
+    results = []
+    for queries, _, _ in batch:
+        rows = queries.shape[0]
+        lane_head = lax.broadcasted_iota(jnp.int32, (rows, LANES), 1) // HEAD
+        halves = []
+        for half in range(queries.shape[1] // LANES):
+            block = mixed.pop(0)
+            result = block[:rows]
+            for head in range(1, group):
+                result = jnp.where(lane_head == head, block[head * rows : (head + 1) * rows], result)
+            halves.append(result)
+        results.append(jnp.concatenate(halves, axis=1))
+    return results
+
+
+def finish_rows(tokens, attended, out_weight, up_weight, down_weight):
+    after = round_trip(tokens + matmul(attended, out_weight))
+    normed = normalise(after).astype(jnp.bfloat16)
+    hidden = jnp.maximum(matmul(normed, up_weight), 0.0).astype(jnp.bfloat16)
+    return round_trip(after + matmul(hidden, down_weight))
+
+
+def core_kernel(
+    place_ref,
+    wave_ref,
+    enc_ref,
+    intra_qkv,
+    intra_out,
+    intra_up,
+    intra_down,
+    inter_qkv,
+    inter_out,
+    inter_up,
+    inter_down,
+    act_ref,
+    own_ref,
+    band32,
+    band,
+    batch,
+    normed,
+    keys,
+    values,
+    query_x,
+    queries,
+    tokens,
+    attended,
+    middle,
+    inter_q,
+    inter_k,
+    inter_v,
+    turned_out,
+    lag,
+):
+    width = enc_ref.shape[1]
+    place = place_ref[0]
+    rows_total = wave_ref.shape[0] - 16
+    segments = rows_total // 8
+    reach = HALF // 2 + HOP
+    spill = LANES - reach
+
+    band32[...] = jnp.zeros_like(band32)
+    filters = enc_ref[...]
+    high = round_trip(filters)
+    low = round_trip(filters - high)
+    for step in range(8):
+        columns = slice(step * width, (step + 1) * width)
+        for piece in range(2):
+            sample = 8 * step + 8 * piece
+            rows = slice(8 * piece, 8 * piece + 8)
+            band32[sample : sample + 8, columns] = high[rows]
+            band32[LANES + sample : LANES + sample + 8, columns] = high[rows]
+            where = LANES + reach + sample if sample < spill else reach + sample - spill
+            band32[where : where + 8, columns] = low[rows]
+    band[...] = band32[...].astype(jnp.bfloat16)
+
+    per_chunk = 64
+    lane = lax.broadcasted_iota(jnp.int32, (per_chunk, LANES), 1)
+
+    def encode_chunk(chunk, carry):
+        start = pl.multiple_of(chunk * per_chunk, per_chunk)
+        here = wave_ref[pl.ds(start, per_chunk), :]
+        after = wave_ref[pl.ds(start + 1, per_chunk), :]
+        turned = jnp.where(lane < 64, pltpu.roll(here, 64, 1), pltpu.roll(after, 64, 1))
+        stacked = []
+        for samples in (here, turned):
+            coarse = round_trip(samples)
+            fine = samples - coarse
+            first = jnp.where(lane < reach, coarse, pltpu.roll(coarse, reach - spill, 1))
+            second = jnp.where(lane < reach, fine, pltpu.roll(coarse, reach, 1))
+            stacked.append(jnp.concatenate([first, second], axis=1))
+        framed = jnp.concatenate(stacked, axis=0).astype(jnp.bfloat16)
+        for step in range(8):
+            columns = slice(step * width, (step + 1) * width)
+            coded = round_trip(jnp.maximum(matmul(framed, band[:, columns]), 0.0))
+            ready = normalise(coded)
+            for half in range(2):
+                rows = slice(half * per_chunk, (half + 1) * per_chunk)
+                batch[8 * half + step] = coded[rows]
+                normed[:, 8 * half + step] = ready[rows].reshape(8, 8, width)
+        query_x[pl.ds(start, per_chunk), :] = batch[place]
+
+        @pl.when(chunk == place)
+        def _():
+            own_ref[...] = batch[...].astype(jnp.bfloat16)
+
+        both = normed[...].reshape(8 * HALF, width).astype(jnp.bfloat16)
+        target = pl.ds(pl.multiple_of(chunk * 8 * HALF, 8 * HALF), 8 * HALF)
+        keys[:, target] = matmul(both, intra_qkv[:, width : 2 * width]).astype(jnp.bfloat16).T
+        values[target, :] = matmul(both, intra_qkv[:, 2 * width :]).astype(jnp.bfloat16)
+        return carry
+
+    lax.fori_loop(0, segments // 8, encode_chunk, 0)
+    keys[:, segments * HALF :] = jnp.zeros((width, HALF), jnp.bfloat16)
+    values[segments * HALF :, :] = jnp.zeros((HALF, width), jnp.bfloat16)
+    query_x[rows_total : rows_total + 8, :] = jnp.zeros((8, width), jnp.float32)
+    queries[rows_total : rows_total + 8, :] = jnp.zeros((8, width), jnp.float32)
+
+    def query_chunk(chunk, carry):
+        rows = pl.ds(pl.multiple_of(chunk * 256, 256), 256)
+        ready = normalise(query_x[rows, :]).astype(jnp.bfloat16)
+        queries[rows, :] = round_trip(matmul(ready, intra_qkv[:, :width]))
+        return carry
+
+    lax.fori_loop(0, rows_total // 256, query_chunk, 0)
+
+    def within_chunk(chunk, carry):
+        batch, targets = [], []
+        for inner in range(WITHIN_BATCH):
+            segment = chunk * WITHIN_BATCH + inner
+            rows = pl.ds(pl.multiple_of(segment * 8, 8), 16)
+            span = pl.ds(pl.multiple_of(segment * HALF, HALF), 2 * HALF)
+            target = pl.ds(pl.multiple_of(segment * 16, 16), 16)
+            tokens[target, :] = query_x[rows, :]
+            batch.append((queries[rows, :], keys.at[:, span], values.at[span, :]))
+            targets.append(target)
+        for target, result in zip(targets, attend_rows(batch)):
+            attended[target, :] = result.astype(jnp.bfloat16)
+        return carry
+
+    lax.fori_loop(0, segments // WITHIN_BATCH, within_chunk, 0)
+
+    positions = 16
+    row_count = positions * segments
+
+    def within_finish(chunk, carry):
+        rows = pl.ds(pl.multiple_of(chunk * 256, 256), 256)
+        put(middle, rows, finish_rows(tokens[rows, :], attended[rows, :], intra_out[...], intra_up[...], intra_down[...]))
+        return carry
+
+    lax.fori_loop(0, row_count // 256, within_finish, 0)
+
+    def turn(chunk, carry):
+        for inner in range(2):
+            spot = chunk * 2 + inner
+            rows = pl.ds(pl.multiple_of(spot * segments, segments), segments)
+            picked = get(middle, pl.ds(spot, segments, stride=positions))
+            tokens[rows, :] = picked
+            triple = matmul(normalise(picked).astype(jnp.bfloat16), inter_qkv[...])
+            inter_q[rows, :] = round_trip(triple[:, :width])
+            inter_k[:, rows] = triple[:, width : 2 * width].astype(jnp.bfloat16).T
+            inter_v[rows, :] = triple[:, 2 * width :].astype(jnp.bfloat16)
+        return carry
+
+    lax.fori_loop(0, positions // 2, turn, 0)
+
+    def across_chunk(spot, carry):
+        rows = pl.ds(pl.multiple_of(spot * segments, segments), segments)
+        (result,) = attend_rows([(inter_q[rows, :], inter_k.at[:, rows], inter_v.at[rows, :])])
+        attended[rows, :] = result.astype(jnp.bfloat16)
+        return carry
+
+    lax.fori_loop(0, positions, across_chunk, 0)
+
+    def across_finish(chunk, carry):
+        rows = pl.ds(pl.multiple_of(chunk * 256, 256), 256)
+        put(middle, rows, finish_rows(tokens[rows, :], attended[rows, :], inter_out[...], inter_up[...], inter_down[...]))
+        return carry
+
+    lax.fori_loop(0, row_count // 256, across_finish, 0)
+
+    lag[0:8, :] = jnp.zeros((8, width), jnp.float32)
+    for spot in range(positions // 2):
+        lag[8 : 8 + segments, :] = get(middle, pl.ds((spot + positions // 2) * segments, segments))
+        combined = round_trip(get(middle, pl.ds(spot * segments, segments)) + lag[7 : 7 + segments, :])
+        active = jnp.where(combined > 0, combined, 0.25 * combined)
+        put(turned_out, pl.ds(spot, segments, stride=positions // 2), active)
+    act_ref[...] = get(turned_out, slice(None)).astype(jnp.bfloat16)
+
+
+def mask_kernel(act_ref, own_ref, weight_ref, out_ref, stage):
+    width = own_ref.shape[-1]
+    steps = own_ref.shape[0]
+    rows = own_ref.shape[1]
+    for step in range(steps):
+        scale = own_ref[step].astype(jnp.float32)
+        for speaker in range(2):
+            columns = slice(speaker * width, (speaker + 1) * width)
+            mask = jnp.maximum(matmul(act_ref[step], weight_ref[:, columns]), 0.0)
+            put(stage, pl.ds(step, rows, stride=steps), mask * scale, speaker)
+    for speaker in range(2):
+        out_ref[speaker] = get(stage.at[speaker], slice(None)).astype(jnp.bfloat16)
+
+
+def core_call(place, wave, enc_weight, *rest):
+    *weights, own_rows = rest
+    width = enc_weight.shape[1]
+    rows_total = wave.shape[0] - 16
+    segments = rows_total // 8
+    row_count = 16 * segments
+    vmem = pl.BlockSpec(memory_space=pltpu.VMEM)
+    return pl.pallas_call(
+        core_kernel,
+        out_shape=(
+            jax.ShapeDtypeStruct((rows_total, width), jnp.bfloat16),
+            jax.ShapeDtypeStruct((16, own_rows, width), jnp.bfloat16),
+        ),
+        in_specs=[pl.BlockSpec(memory_space=pltpu.SMEM)] + [vmem] * 10,
+        out_specs=(vmem, vmem),
+        scratch_shapes=[
+            pltpu.VMEM((2 * LANES, 8 * width), jnp.float32),
+            pltpu.VMEM((2 * LANES, 8 * width), jnp.bfloat16),
+            pltpu.VMEM((16, own_rows, width), jnp.float32),
+            pltpu.VMEM((8, 16, 8, width), jnp.float32),
+            pltpu.VMEM((width, (segments + 1) * HALF), jnp.bfloat16),
+            pltpu.VMEM(((segments + 1) * HALF, width), jnp.bfloat16),
+            pltpu.VMEM((rows_total + 8, width), jnp.float32),
+            pltpu.VMEM((rows_total + 8, width), jnp.float32),
+            pltpu.VMEM((row_count, width), jnp.float32),
+            pltpu.VMEM((row_count, width), jnp.bfloat16),
+            pltpu.VMEM((width // LANES, row_count, LANES), jnp.float32),
+            pltpu.VMEM((row_count, width), jnp.float32),
+            pltpu.VMEM((width, row_count), jnp.bfloat16),
+            pltpu.VMEM((row_count, width), jnp.bfloat16),
+            pltpu.VMEM((width // LANES, rows_total, LANES), jnp.float32),
+            pltpu.VMEM((segments + 8, width), jnp.float32),
+        ],
+        compiler_params=pltpu.CompilerParams(vmem_limit_bytes=60 * 1024 * 1024),
+        name="core",
+    )(place, wave, enc_weight, *weights)
+
+
+def gather_doubling(value, axis):
+    count = lax.axis_size(axis)
+    index = lax.axis_index(axis)
+    held = value[None]
+    bit = count // 2
+    while bit:
+        other = lax.ppermute(held, axis, [(source, source ^ bit) for source in range(count)])
+        upper = (index // bit) % 2
+        first = jnp.where(upper == 0, held, other)
+        second = jnp.where(upper == 0, other, held)
+        held = jnp.stack([first, second], axis=1).reshape((-1,) + value.shape)
+        bit //= 2
+    return held.reshape((-1,) + value.shape[1:])
+
+
+def local_gathered(
+    waveform,
+    enc_weight,
+    intra_qkv,
+    intra_out,
+    intra_up,
+    intra_down,
+    inter_qkv,
+    inter_out,
+    inter_up,
+    inter_down,
+    mask_weight,
+):
+    width = enc_weight.shape[1]
+    count = lax.axis_size("tm")
+    samples = waveform.reshape(-1, LANES)
+    gathered = gather_doubling(samples, "tm")
+    wave = jnp.concatenate([gathered, jnp.zeros((16, LANES), jnp.float32)], axis=0)
+    own_rows = samples.shape[0]
+    place = lax.axis_index("tm").reshape(1)
+    weights = (intra_qkv, intra_out, intra_up, intra_down, inter_qkv, inter_out, inter_up, inter_down)
+    act, own = core_call(place, wave, enc_weight, *weights, own_rows)
+    pieces = act.reshape(count, own_rows, width)
+    vmem = pl.BlockSpec(memory_space=pltpu.VMEM)
+    received = lax.all_to_all(pieces, "tm", split_axis=0, concat_axis=0, tiled=True)
+    return pl.pallas_call(
+        mask_kernel,
+        out_shape=jax.ShapeDtypeStruct((2, 16 * own_rows, width), jnp.bfloat16),
+        in_specs=[vmem] * 3,
+        out_specs=vmem,
+        scratch_shapes=[pltpu.VMEM((2, width // LANES, 16 * own_rows, LANES), jnp.float32)],
+        compiler_params=pltpu.CompilerParams(vmem_limit_bytes=32 * 1024 * 1024),
+        name="mask",
+    )(received, own, mask_weight)
+
+
 def solution(mesh):
+    body = local_gathered if mesh.shape["tm"] == 16 else local
     return jax.shard_map(
-        local,
+        body,
         mesh=mesh,
         in_specs=(P(("grp", "tm")), P(), P(), P(), P(), P(), P(), P(), P(), P(), P()),
         out_specs=P(None, ("grp", "tm"), None),

time: 152 us -> 106 us (0.70); the launches traced: 149 us -> 106 us
  Pallas kernels: 0 us -> 67 us
  matrix products: 43.4 us -> 0 us
  blocking collectives: 63.1 us -> 20.5 us
  local copies, waits for them, and re-layouts: 23.3 us -> 0.84 us
  other arithmetic: 8.87 us -> 0.17 us
  waiting for transfers between devices: 4.61 us -> 10.1 us
  starting transfers between devices: 5.58 us -> 7.43 us
    pallas_call x0 -> x2, Pallas kernels: none -> 67 us  [the longest x1 64.4 us: core_call(): pl.pallas_call(core_kernel, out_shape=(jax.ShapeDtypeStruct((rows_total,...]
    all_to_all x2 -> x1, blocking collectives: 63.1 us -> 20.5 us  [local_gathered(): lax.all_to_all(pieces, 'tm', split_axis=0, concat_axis=0, tiled=True)]
    dot_general x10 -> x0, matrix products: 25 us -> none  [the longest x2 12 us: attend(): jnp.einsum(weigh_form, probs, value_heads, preferred_element_type=jnp.flo...]
    sub x2 -> x0, matrix products: 18.4 us -> none  [attend(): probs = jax.nn.softmax(scores, axis=-1).astype(jnp.bfloat16)]
    slice x13 -> x0, local copies, waits for them, and re-layouts: 17.2 us -> none  [the longest x4 7.96 us: transformer_layer(): triple[..., model_width:2 * model_width]]
    ppermute x3 -> x4, waiting for transfers between devices: 4.61 us -> 10.1 us  [gather_doubling(): lax.ppermute(held, axis, [(source, source ^ bit) for source in range(coun...]
    reshape x5 -> x0, local copies, waits for them, and re-layouts: 4.8 us -> none  [the longest x1 1.92 us: local(): mask_values = mask_values.reshape(frames_here, 2, model_width)]
    reduce_sum x8 -> x0, other arithmetic: 3.94 us -> none  [the longest x4 2.57 us: layer_norm(): spread = jnp.mean(centred * centred, axis=-1, keepdims=True)]
  transfers between devices with their start and end apart: 3 -> 4, of which waited for: 2 -> 4; matrix products, arithmetic and copies ran while one was open for 2% -> 0% of each run, Pallas kernels for 0% -> 0%
where the time goes in v1:
time: 106 us
  Pallas kernels  67 us (63%)
  blocking collectives  20.5 us (19%)
  waiting for transfers between devices  10.1 us (10%)
  starting transfers between devices  7.43 us (7%)
    pallas_call x1, Pallas kernels, core_call(): pl.pallas_call(core_kernel, out_shape=(jax.ShapeDtypeStruct((rows_total,...  64.4 us
    all_to_all x1, blocking collectives, local_gathered(): lax.all_to_all(pieces, 'tm', split_axis=0, concat_axis=0, tiled=True)  20.5 us
    ppermute x4, waiting for transfers between devices, gather_doubling(): lax.ppermute(held, axis, [(source, source ^ bit) for source in range(coun...  10.1 us
    ppermute x4, starting transfers between devices, gather_doubling(): lax.ppermute(held, axis, [(source, source ^ bit) for source in range(coun...  7.43 us
    pallas_call x1, Pallas kernels, local_gathered(): pl.pallas_call(mask_kernel, out_shape=jax.ShapeDtypeStruct((2, 16 * own_r...  2.62 us
  transfers between devices with their start and end apart: 4, of which 4 were waited for; matrix products, arithmetic and copies ran while one was open for 0% of the time, Pallas kernels for 0%

profile of v1, /device:TPU:0, one launch (start us, length us, event | category | flops | bytes accessed | tf_op | source)
XLA Modules:
  0.0 106.2 jit_solution(4106247190649819533)
XLA Ops:
  0.0 0.0 copy-start.2
  0.0 4.1 %collective-permute-start = (f32[1,64,128]{2,1,0:T(8,128)}, f32[1,64,128]{2,1,0:T(8,128)S(1)}, u32[]{:S(2)}, u32[]{:S(2)}) collective-permute-start(f32[1,64,128]{2,1,0:T(8,128)} %bitcast.44), channel_id=1, source_target_pairs={{0,8},{1,9},{2,10},{3,11},{4,12},{5,13},{6,14},{7,15},{8,0},{9,1},... | collective-permute-start | bytes 98312 | tf_op jit(solution)/shard_map/ppermute | solution.py:430
  4.1 2.5 %collective-permute-done = f32[1,64,128]{2,1,0:T(8,128)S(1)} collective-permute-done((f32[1,64,128]{2,1,0:T(8,128)}, f32[1,64,128]{2,1,0:T(8,128)S(1)}, u32[]{:S(2)}, u32[]{:S(2)}) %collective-permute-start) | collective-permute-done | bytes 32800 | tf_op jit(solution)/shard_map/ppermute | solution.py:430
  6.6 0.0 copy-done.2
  6.6 1.6 %collective-permute-start.1 = (f32[2,64,128]{2,1,0:T(8,128)S(1)}, f32[2,64,128]{2,1,0:T(8,128)S(1)}, u32[]{:S(2)}, u32[]{:S(2)}) collective-permute-start(f32[2,64,128]{2,1,0:T(8,128)S(1)} %maximum_bitcast_fusion), channel_id=1, source_target_pairs={{0,4},{1,5},{2,6},{3,7},{4,0},{5,1},{6,2},{7,3},{8,12},{9,13},{10,... | collective-permute-start | bytes 196616 | tf_op jit(solution)/shard_map/ppermute | solution.py:430
  8.2 2.8 %collective-permute-done.1 = f32[2,64,128]{2,1,0:T(8,128)S(1)} collective-permute-done((f32[2,64,128]{2,1,0:T(8,128)S(1)}, f32[2,64,128]{2,1,0:T(8,128)S(1)}, u32[]{:S(2)}, u32[]{:S(2)}) %collective-permute-start.1) | collective-permute-done | bytes 65568 | tf_op jit(solution)/shard_map/ppermute | solution.py:430
  11.0 1.7 %collective-permute-start.2 = (f32[4,64,128]{2,1,0:T(8,128)S(1)}, f32[4,64,128]{2,1,0:T(8,128)S(1)}, u32[]{:S(2)}, u32[]{:S(2)}) collective-permute-start(f32[4,64,128]{2,1,0:T(8,128)S(1)} %bitcast.42), channel_id=1, source_target_pairs={{0,2},{1,3},{2,0},{3,1},{4,6},{5,7},{6,4},{7,5},{8,10},{9,11},{10,... | collective-permute-start | bytes 393224 | tf_op jit(solution)/shard_map/ppermute | solution.py:430
  12.7 3.3 %collective-permute-done.2 = f32[4,64,128]{2,1,0:T(8,128)S(1)} collective-permute-done((f32[4,64,128]{2,1,0:T(8,128)S(1)}, f32[4,64,128]{2,1,0:T(8,128)S(1)}, u32[]{:S(2)}, u32[]{:S(2)}) %collective-permute-start.2) | collective-permute-done | bytes 131104 | tf_op jit(solution)/shard_map/ppermute | solution.py:430
  16.1 0.1 collective-permute-start.3
  16.2 1.5 %collective-permute-done.3 = f32[8,64,128]{2,1,0:T(8,128)S(1)} collective-permute-done((f32[8,64,128]{2,1,0:T(8,128)S(1)}, f32[8,64,128]{2,1,0:T(8,128)S(1)}, u32[]{:S(2)}, u32[]{:S(2)}) %collective-permute-start.3) | collective-permute-done | bytes 262176 | tf_op jit(solution)/shard_map/ppermute | solution.py:430
  17.7 0.1 select_bitcast_fusion.1
  17.8 0.8 concatenate.3.wave_ref
  18.6 64.4 %core.1 = (bf16[1024,256]{1,0:T(8,128)(2,1)}, bf16[16,64,256]{2,1,0:T(8,128)(2,1)}) custom-call(s32[1]{0:T(128)} %bitcast.place_ref, f32[1040,128]{1,0:T(8,128)} %concatenate.3.wave_ref, f32[16,256]{1,0:T(8,128)} %enc_ref.1, bf16[256,768]{1,0:T(8,128)(2,1)} %intra_qkv.1, bf16[256,256]{1,0:T(8,128)(2,1)} %intra_out.1, bf16[256,1024]{1,0:T(8,128)(2,1)} %intra_up.1, ...), custom_call_target="tpu_custom_call" | custom-call | tf_op jit(solution)/shard_map/core/pallas_call | solution.py:393
  83.0 0.0 copy-start
  83.0 0.0 copy-start.1
  83.1 20.5 %all_to_all.5.act_ref = bf16[16,64,256]{2,1,0:T(8,128)(2,1)S(1)} all-to-all(bf16[16,64,256]{2,1,0:T(8,128)(2,1)} %bitcast.43), channel_id=1, replica_groups=mesh['grp'=2,'tm'=16] {'tm'}, dimensions={0} | all-to-all | bytes 1048576 | tf_op jit(solution)/shard_map/all_to_all | solution.py:463
  103.5 0.0 copy-done
  103.6 0.0 copy-done.1
  103.6 2.6 %mask.1 = bf16[2,1024,256]{2,1,0:T(8,128)(2,1)} custom-call(bf16[16,64,256]{2,1,0:T(8,128)(2,1)S(1)} %all_to_all.5.act_ref, bf16[16,64,256]{2,1,0:T(8,128)(2,1)S(1)} %copy-done, bf16[256,512]{1,0:T(8,128)(2,1)S(1)} %copy-done.1), custom_call_target="tpu_custom_call" | custom-call | tf_op jit(solution)/shard_map/mask/pallas_call | solution.py:464
  (7 shorter events, 0.1 us)
Async XLA Ops:
  0.0 6.6 %copy-start.2 = (f32[8192]{0:T(1024)S(1)}, f32[8192]{0:T(1024)}, u32[]{:S(2)}) copy-start(f32[8192]{0:T(1024)} %param.11) | copy-start | bytes 98308
  0.0 6.6 %collective-permute-start = (f32[1,64,128]{2,1,0:T(8,128)}, f32[1,64,128]{2,1,0:T(8,128)S(1)}, u32[]{:S(2)}, u32[]{:S(2)}) collective-permute-start(f32[1,64,128]{2,1,0:T(8,128)} %bitcast.44), channel_id=1, source_target_pairs={{0,8},{1,9},{2,10},{3,11},{4,12},{5,13},{6,14},{7,15},{8,0},{9,1},... | collective-permute-start | bytes 98312 | tf_op jit(solution)/shard_map/ppermute | solution.py:430
  6.6 4.3 %collective-permute-start.1 = (f32[2,64,128]{2,1,0:T(8,128)S(1)}, f32[2,64,128]{2,1,0:T(8,128)S(1)}, u32[]{:S(2)}, u32[]{:S(2)}) collective-permute-start(f32[2,64,128]{2,1,0:T(8,128)S(1)} %maximum_bitcast_fusion), channel_id=1, source_target_pairs={{0,4},{1,5},{2,6},{3,7},{4,0},{5,1},{6,2},{7,3},{8,12},{9,13},{10,... | collective-permute-start | bytes 196616 | tf_op jit(solution)/shard_map/ppermute | solution.py:430
  11.0 5.0 %collective-permute-start.2 = (f32[4,64,128]{2,1,0:T(8,128)S(1)}, f32[4,64,128]{2,1,0:T(8,128)S(1)}, u32[]{:S(2)}, u32[]{:S(2)}) collective-permute-start(f32[4,64,128]{2,1,0:T(8,128)S(1)} %bitcast.42), channel_id=1, source_target_pairs={{0,2},{1,3},{2,0},{3,1},{4,6},{5,7},{6,4},{7,5},{8,10},{9,11},{10,... | collective-permute-start | bytes 393224 | tf_op jit(solution)/shard_map/ppermute | solution.py:430
  16.1 1.6 %collective-permute-start.3 = (f32[8,64,128]{2,1,0:T(8,128)S(1)}, f32[8,64,128]{2,1,0:T(8,128)S(1)}, u32[]{:S(2)}, u32[]{:S(2)}) collective-permute-start(f32[8,64,128]{2,1,0:T(8,128)S(1)} %bitcast.41), channel_id=1, source_target_pairs={{0,1},{1,0},{2,3},{3,2},{4,5},{5,4},{6,7},{7,6},{8,9},{9,8},{10,11... | collective-permute-start | bytes 786440 | tf_op jit(solution)/shard_map/ppermute | solution.py:430
  83.0 20.5 %copy-start = (bf16[16,64,256]{2,1,0:T(8,128)(2,1)S(1)}, bf16[16,64,256]{2,1,0:T(8,128)(2,1)}, u32[]{:S(2)}) copy-start(bf16[16,64,256]{2,1,0:T(8,128)(2,1)} %get-tuple-element.8.own_ref) | copy-start | bytes 1572868
  83.0 20.5 %copy-start.1 = (bf16[256,512]{1,0:T(8,128)(2,1)S(1)}, bf16[256,512]{1,0:T(8,128)(2,1)}, u32[]{:S(2)}) copy-start(bf16[256,512]{1,0:T(8,128)(2,1)} %weight_ref.1) | copy-start | bytes 786436

commit v2 on v1

--- a/solution.py
+++ b/solution.py
@@ -135,6 +135,10 @@
 
 LANES = 128
 WITHIN_BATCH = 4
+ACROSS_BATCH = 2
+FINISH_ROWS = 1024
+ENCODE_BLOCKS = 16
+TURN_BATCH = 4
 SCORE_SCALE = math.log2(math.e) * HEAD ** (-0.5)
 
 
@@ -153,9 +157,9 @@
     return jnp.dot(left, right, preferred_element_type=jnp.float32)
 
 
-def put(ref, rows, value, *lead):
+def put(ref, rows, value):
     for block in range(value.shape[1] // LANES):
-        ref[(*lead, block, rows, slice(None))] = value[:, block * LANES : (block + 1) * LANES]
+        ref[block, rows, :] = value[:, block * LANES : (block + 1) * LANES]
 
 
 def get(ref, rows):
@@ -195,6 +199,38 @@
     return results
 
 
+def attend_paired(batch):
+    group = LANES // HEAD
+    work = []
+    for queries, keys, values in batch:
+        lane_head = lax.broadcasted_iota(jnp.int32, queries.shape, 1) % LANES // HEAD
+        spread = [jnp.where(lane_head == head, queries, 0.0) for head in range(group)]
+        work.append(matmul(jnp.concatenate(spread, axis=0).astype(jnp.bfloat16), keys[...]))
+    staged = []
+    for scores in work:
+        weights, shares = [], []
+        for half in range(2):
+            part = scores[:, half * LANES : (half + 1) * LANES]
+            part = jnp.exp2((part - jnp.max(part, axis=-1, keepdims=True)) * SCORE_SCALE)
+            weights.append(part.astype(jnp.bfloat16))
+            shares.append(1.0 / jnp.sum(part, axis=-1, keepdims=True))
+        staged.append((jnp.concatenate(weights, axis=1), shares))
+    results = []
+    for (queries, keys, values), (weights, shares) in zip(batch, staged):
+        rows = queries.shape[0]
+        lane_head = lax.broadcasted_iota(jnp.int32, (rows, LANES), 1) // HEAD
+        mixed = matmul(weights, values[...])
+        halves = []
+        for half in range(2):
+            block = mixed[:, half * LANES : (half + 1) * LANES] * shares[half]
+            result = block[:rows]
+            for head in range(1, group):
+                result = jnp.where(lane_head == head, block[head * rows : (head + 1) * rows], result)
+            halves.append(result)
+        results.append(jnp.concatenate(halves, axis=1))
+    return results
+
+
 def finish_rows(tokens, attended, out_weight, up_weight, down_weight):
     after = round_trip(tokens + matmul(attended, out_weight))
     normed = normalise(after).astype(jnp.bfloat16)
@@ -204,22 +240,51 @@
 
 def core_kernel(
     place_ref,
+    near_ref,
+    far_ref,
+    enc_ref,
+    *rest,
+):
+    weight_sources, rest = rest[:8], rest[8:]
+    act_ref, own_ref, rest = rest[0], rest[1], rest[2:]
+    weight_buffers, arrivals, wave_ref, wave_arrivals, rest = rest[:8], rest[8], rest[9], rest[10], rest[11:]
+    place = place_ref[0]
+    chunk_rows = near_ref.shape[1]
+    moves = []
+    for slot in range(16):
+        source = near_ref if slot < 8 else far_ref
+        along = (place // 4 + slot % 4) % 4
+        flipped = (place // 2 + (slot // 4) % 2) % 2
+        owner = along * 4 + flipped * 2 + (place + slot // 8) % 2
+        target = wave_ref.at[pl.ds(pl.multiple_of(owner * chunk_rows, chunk_rows), chunk_rows), :]
+        moves.append(pltpu.make_async_copy(source.at[slot % 8], target, wave_arrivals.at[slot]))
+    for move in moves:
+        move.start()
+    tail = wave_ref.shape[0] - 16
+    wave_ref[tail:, :] = jnp.zeros((16, LANES), jnp.float32)
+    copies = [
+        pltpu.make_async_copy(source, buffer, arrivals.at[index])
+        for index, (source, buffer) in enumerate(zip(weight_sources, weight_buffers))
+    ]
+    for copy in copies:
+        copy.start()
+    waits = [copy.wait for copy in copies] + [move.wait for move in moves]
+    core_body(place, wave_ref, enc_ref, weight_buffers, waits, act_ref, own_ref, *rest)
+
+
+def core_body(
+    place,
     wave_ref,
     enc_ref,
-    intra_qkv,
-    intra_out,
-    intra_up,
-    intra_down,
-    inter_qkv,
-    inter_out,
-    inter_up,
-    inter_down,
+    weights,
+    ready_waits,
     act_ref,
     own_ref,
     band32,
     band,
-    batch,
+    framed,
     normed,
+    normed_next,
     keys,
     values,
     query_x,
@@ -233,8 +298,8 @@
     turned_out,
     lag,
 ):
+    intra_qkv, intra_out, intra_up, intra_down, inter_qkv, inter_out, inter_up, inter_down = weights
     width = enc_ref.shape[1]
-    place = place_ref[0]
     rows_total = wave_ref.shape[0] - 16
     segments = rows_total // 8
     reach = HALF // 2 + HOP
@@ -253,57 +318,79 @@
             band32[LANES + sample : LANES + sample + 8, columns] = high[rows]
             where = LANES + reach + sample if sample < spill else reach + sample - spill
             band32[where : where + 8, columns] = low[rows]
-    band[...] = band32[...].astype(jnp.bfloat16)
-
-    per_chunk = 64
+    for step in range(8):
+        band[step] = band32[:, step * width : (step + 1) * width].astype(jnp.bfloat16)
+
+    per_chunk = 8 * ENCODE_BLOCKS
     lane = lax.broadcasted_iota(jnp.int32, (per_chunk, LANES), 1)
-
-    def encode_chunk(chunk, carry):
+    chunk_frames = ENCODE_BLOCKS * HALF
+    quarter = chunk_frames // 2
+
+    def encode_chunk(chunk, fill, drain):
         start = pl.multiple_of(chunk * per_chunk, per_chunk)
         here = wave_ref[pl.ds(start, per_chunk), :]
         after = wave_ref[pl.ds(start + 1, per_chunk), :]
         turned = jnp.where(lane < 64, pltpu.roll(here, 64, 1), pltpu.roll(after, 64, 1))
         stacked = []
-        for samples in (here, turned):
+        for half, samples in enumerate((here, turned)):
             coarse = round_trip(samples)
             fine = samples - coarse
             first = jnp.where(lane < reach, coarse, pltpu.roll(coarse, reach - spill, 1))
             second = jnp.where(lane < reach, fine, pltpu.roll(coarse, reach, 1))
-            stacked.append(jnp.concatenate([first, second], axis=1))
-        framed = jnp.concatenate(stacked, axis=0).astype(jnp.bfloat16)
-        for step in range(8):
-            columns = slice(step * width, (step + 1) * width)
-            coded = round_trip(jnp.maximum(matmul(framed, band[:, columns]), 0.0))
-            ready = normalise(coded)
+            packed = jnp.concatenate([first, second], axis=1).astype(jnp.bfloat16)
+            framed[half, pl.ds(start, per_chunk), :] = packed
+            stacked.append(packed)
+        rows_in = jnp.concatenate(stacked, axis=0)
+        for step in range(0, 8, 2):
+            if drain is not None and step % 4 == 0:
+                project(chunk - 1, drain, step // 4)
+            pair = [normalise(jnp.maximum(matmul(rows_in, band[step + side]), 0.0)) for side in range(2)]
             for half in range(2):
-                rows = slice(half * per_chunk, (half + 1) * per_chunk)
-                batch[8 * half + step] = coded[rows]
-                normed[:, 8 * half + step] = ready[rows].reshape(8, 8, width)
-        query_x[pl.ds(start, per_chunk), :] = batch[place]
-
-        @pl.when(chunk == place)
-        def _():
-            own_ref[...] = batch[...].astype(jnp.bfloat16)
-
-        both = normed[...].reshape(8 * HALF, width).astype(jnp.bfloat16)
-        target = pl.ds(pl.multiple_of(chunk * 8 * HALF, 8 * HALF), 8 * HALF)
+                for block in range(ENCODE_BLOCKS):
+                    rows = slice(half * per_chunk + 8 * block, half * per_chunk + 8 * block + 8)
+                    tile = jnp.concatenate([pair[0][rows], pair[1][rows]], axis=0).astype(jnp.bfloat16)
+                    spot = block * HALF + (8 * half + step) * 8
+                    fill[spot : spot + 16, :] = tile
+
+    def project(chunk, drain, part):
+        both = drain[part * quarter : (part + 1) * quarter, :]
+        target = pl.ds(pl.multiple_of(chunk * chunk_frames + part * quarter, quarter), quarter)
         keys[:, target] = matmul(both, intra_qkv[:, width : 2 * width]).astype(jnp.bfloat16).T
         values[target, :] = matmul(both, intra_qkv[:, 2 * width :]).astype(jnp.bfloat16)
+
+    for wait in ready_waits[8:]:
+        wait()
+    ready_waits[0]()
+
+    def query_rows(part):
+        rows = slice(part * rows_total // 2, (part + 1) * rows_total // 2)
+        coded = round_trip(jnp.maximum(matmul(framed[place // 8, rows, :], band[place % 8]), 0.0))
+        query_x[rows, :] = coded
+        queries[rows, :] = round_trip(matmul(normalise(coded).astype(jnp.bfloat16), intra_qkv[:, :width]))
+
+    chunks = segments // ENCODE_BLOCKS
+    encode_chunk(0, normed, None)
+
+    def encode_pair(index, carry):
+        encode_chunk(2 * index + 1, normed_next, normed)
+        encode_chunk(2 * index + 2, normed, normed_next)
         return carry
 
-    lax.fori_loop(0, segments // 8, encode_chunk, 0)
+    lax.fori_loop(0, (chunks - 1) // 2, encode_pair, 0)
+    encode_chunk(chunks - 1, normed_next, normed)
+    for part in range(2):
+        query_rows(part)
+        project(chunks - 1, normed_next, part)
     keys[:, segments * HALF :] = jnp.zeros((width, HALF), jnp.bfloat16)
     values[segments * HALF :, :] = jnp.zeros((HALF, width), jnp.bfloat16)
     query_x[rows_total : rows_total + 8, :] = jnp.zeros((8, width), jnp.float32)
     queries[rows_total : rows_total + 8, :] = jnp.zeros((8, width), jnp.float32)
-
-    def query_chunk(chunk, carry):
-        rows = pl.ds(pl.multiple_of(chunk * 256, 256), 256)
-        ready = normalise(query_x[rows, :]).astype(jnp.bfloat16)
-        queries[rows, :] = round_trip(matmul(ready, intra_qkv[:, :width]))
-        return carry
-
-    lax.fori_loop(0, rows_total // 256, query_chunk, 0)
+    own_rows = own_ref.shape[1]
+    rows = pl.ds(pl.multiple_of(place * own_rows, own_rows), own_rows)
+    for half in range(2):
+        mine = framed[half, rows, :]
+        for step in range(8):
+            own_ref[8 * half + step] = jnp.maximum(matmul(mine, band[step]), 0.0).astype(jnp.bfloat16)
 
     def within_chunk(chunk, carry):
         batch, targets = [], []
@@ -324,41 +411,65 @@
     positions = 16
     row_count = positions * segments
 
+    for index in (1, 2, 3):
+        ready_waits[index]()
+
     def within_finish(chunk, carry):
-        rows = pl.ds(pl.multiple_of(chunk * 256, 256), 256)
+        rows = pl.ds(pl.multiple_of(chunk * FINISH_ROWS, FINISH_ROWS), FINISH_ROWS)
         put(middle, rows, finish_rows(tokens[rows, :], attended[rows, :], intra_out[...], intra_up[...], intra_down[...]))
         return carry
 
-    lax.fori_loop(0, row_count // 256, within_finish, 0)
+    lax.fori_loop(0, row_count // FINISH_ROWS, within_finish, 0)
+
+    for index in (4, 5, 6, 7):
+        ready_waits[index]()
+    for half in range(2):
+        part = slice(half * LANES, (half + 1) * LANES)
+        span = slice((1 - half) * segments, (2 - half) * segments)
+        inter_k[:, part, span] = jnp.zeros((positions, LANES, segments), jnp.bfloat16)
+        inter_v[:, span, part] = jnp.zeros((positions, segments, LANES), jnp.bfloat16)
 
     def turn(chunk, carry):
-        for inner in range(2):
-            spot = chunk * 2 + inner
+        rows = pl.ds(pl.multiple_of(chunk * TURN_BATCH * segments, TURN_BATCH * segments), TURN_BATCH * segments)
+        for inner in range(TURN_BATCH):
+            spot = chunk * TURN_BATCH + inner
+            target = pl.ds(pl.multiple_of(spot * segments, segments), segments)
+            tokens[target, :] = get(middle, pl.ds(spot, segments, stride=positions))
+        ready = normalise(tokens[rows, :]).astype(jnp.bfloat16)
+        inter_q[rows, :] = round_trip(matmul(ready, inter_qkv[:, :width]))
+        turned_keys = matmul(ready, inter_qkv[:, width : 2 * width]).astype(jnp.bfloat16).T
+        new_values = matmul(ready, inter_qkv[:, 2 * width :]).astype(jnp.bfloat16)
+        for inner in range(TURN_BATCH):
+            spot = chunk * TURN_BATCH + inner
+            source = slice(inner * segments, (inner + 1) * segments)
+            for half in range(2):
+                part = slice(half * LANES, (half + 1) * LANES)
+                span = slice(half * segments, (half + 1) * segments)
+                inter_k[spot, part, span] = turned_keys[part, source]
+                inter_v[spot, span, part] = new_values[source, part]
+        return carry
+
+    lax.fori_loop(0, positions // TURN_BATCH, turn, 0)
+
+    def across_chunk(chunk, carry):
+        batch, targets = [], []
+        for inner in range(ACROSS_BATCH):
+            spot = chunk * ACROSS_BATCH + inner
             rows = pl.ds(pl.multiple_of(spot * segments, segments), segments)
-            picked = get(middle, pl.ds(spot, segments, stride=positions))
-            tokens[rows, :] = picked
-            triple = matmul(normalise(picked).astype(jnp.bfloat16), inter_qkv[...])
-            inter_q[rows, :] = round_trip(triple[:, :width])
-            inter_k[:, rows] = triple[:, width : 2 * width].astype(jnp.bfloat16).T
-            inter_v[rows, :] = triple[:, 2 * width :].astype(jnp.bfloat16)
+            batch.append((inter_q[rows, :], inter_k.at[spot], inter_v.at[spot]))
+            targets.append(rows)
+        for target, result in zip(targets, attend_paired(batch)):
+            attended[target, :] = result.astype(jnp.bfloat16)
         return carry
 
-    lax.fori_loop(0, positions // 2, turn, 0)
-
-    def across_chunk(spot, carry):
-        rows = pl.ds(pl.multiple_of(spot * segments, segments), segments)
-        (result,) = attend_rows([(inter_q[rows, :], inter_k.at[:, rows], inter_v.at[rows, :])])
-        attended[rows, :] = result.astype(jnp.bfloat16)
-        return carry
-
-    lax.fori_loop(0, positions, across_chunk, 0)
+    lax.fori_loop(0, positions // ACROSS_BATCH, across_chunk, 0)
 
     def across_finish(chunk, carry):
-        rows = pl.ds(pl.multiple_of(chunk * 256, 256), 256)
+        rows = pl.ds(pl.multiple_of(chunk * FINISH_ROWS, FINISH_ROWS), FINISH_ROWS)
         put(middle, rows, finish_rows(tokens[rows, :], attended[rows, :], inter_out[...], inter_up[...], inter_down[...]))
         return carry
 
-    lax.fori_loop(0, row_count // 256, across_finish, 0)
+    lax.fori_loop(0, row_count // FINISH_ROWS, across_finish, 0)
 
     lag[0:8, :] = jnp.zeros((8, width), jnp.float32)
     for spot in range(positions // 2):
@@ -370,39 +481,39 @@
 
 
 def mask_kernel(act_ref, own_ref, weight_ref, out_ref, stage):
-    width = own_ref.shape[-1]
-    steps = own_ref.shape[0]
-    rows = own_ref.shape[1]
+    steps, rows, _ = own_ref.shape
     for step in range(steps):
-        scale = own_ref[step].astype(jnp.float32)
-        for speaker in range(2):
-            columns = slice(speaker * width, (speaker + 1) * width)
-            mask = jnp.maximum(matmul(act_ref[step], weight_ref[:, columns]), 0.0)
-            put(stage, pl.ds(step, rows, stride=steps), mask * scale, speaker)
-    for speaker in range(2):
-        out_ref[speaker] = get(stage.at[speaker], slice(None)).astype(jnp.bfloat16)
-
-
-def core_call(place, wave, enc_weight, *rest):
-    *weights, own_rows = rest
+        mask = jnp.maximum(matmul(act_ref[step], weight_ref[...]), 0.0)
+        put(stage, pl.ds(step, rows, stride=steps), mask * own_ref[step].astype(jnp.float32))
+    out_ref[0] = get(stage, slice(None)).astype(jnp.bfloat16)
+
+
+def core_call(place, near, far, enc_weight, *weights):
     width = enc_weight.shape[1]
-    rows_total = wave.shape[0] - 16
+    own_rows = near.shape[1]
+    rows_total = 2 * near.shape[0] * own_rows
     segments = rows_total // 8
     row_count = 16 * segments
     vmem = pl.BlockSpec(memory_space=pltpu.VMEM)
+    anywhere = pl.BlockSpec(memory_space=pl.ANY)
     return pl.pallas_call(
         core_kernel,
         out_shape=(
             jax.ShapeDtypeStruct((rows_total, width), jnp.bfloat16),
             jax.ShapeDtypeStruct((16, own_rows, width), jnp.bfloat16),
         ),
-        in_specs=[pl.BlockSpec(memory_space=pltpu.SMEM)] + [vmem] * 10,
+        in_specs=[pl.BlockSpec(memory_space=pltpu.SMEM)] + [anywhere] * 2 + [vmem] + [anywhere] * 8,
         out_specs=(vmem, vmem),
-        scratch_shapes=[
+        scratch_shapes=[pltpu.VMEM(weight.shape, weight.dtype) for weight in weights]
+        + [
+            pltpu.SemaphoreType.DMA((8,)),
+            pltpu.VMEM((rows_total + 16, LANES), jnp.float32),
+            pltpu.SemaphoreType.DMA((16,)),
             pltpu.VMEM((2 * LANES, 8 * width), jnp.float32),
-            pltpu.VMEM((2 * LANES, 8 * width), jnp.bfloat16),
-            pltpu.VMEM((16, own_rows, width), jnp.float32),
-            pltpu.VMEM((8, 16, 8, width), jnp.float32),
+            pltpu.VMEM((8, 2 * LANES, width), jnp.bfloat16),
+            pltpu.VMEM((2, rows_total, 2 * LANES), jnp.bfloat16),
+            pltpu.VMEM((ENCODE_BLOCKS * HALF, width), jnp.bfloat16),
+            pltpu.VMEM((ENCODE_BLOCKS * HALF, width), jnp.bfloat16),
             pltpu.VMEM((width, (segments + 1) * HALF), jnp.bfloat16),
             pltpu.VMEM(((segments + 1) * HALF, width), jnp.bfloat16),
             pltpu.VMEM((rows_total + 8, width), jnp.float32),
@@ -411,29 +522,24 @@
             pltpu.VMEM((row_count, width), jnp.bfloat16),
             pltpu.VMEM((width // LANES, row_count, LANES), jnp.float32),
             pltpu.VMEM((row_count, width), jnp.float32),
-            pltpu.VMEM((width, row_count), jnp.bfloat16),
-            pltpu.VMEM((row_count, width), jnp.bfloat16),
+            pltpu.VMEM((16, width, 2 * segments), jnp.bfloat16),
+            pltpu.VMEM((16, 2 * segments, width), jnp.bfloat16),
             pltpu.VMEM((width // LANES, rows_total, LANES), jnp.float32),
             pltpu.VMEM((segments + 8, width), jnp.float32),
         ],
         compiler_params=pltpu.CompilerParams(vmem_limit_bytes=60 * 1024 * 1024),
         name="core",
-    )(place, wave, enc_weight, *weights)
-
-
-def gather_doubling(value, axis):
+    )(place, near, far, enc_weight, *weights)
+
+
+def gather_chunks(value, axis):
     count = lax.axis_size(axis)
-    index = lax.axis_index(axis)
-    held = value[None]
-    bit = count // 2
-    while bit:
-        other = lax.ppermute(held, axis, [(source, source ^ bit) for source in range(count)])
-        upper = (index // bit) % 2
-        first = jnp.where(upper == 0, held, other)
-        second = jnp.where(upper == 0, other, held)
-        held = jnp.stack([first, second], axis=1).reshape((-1,) + value.shape)
-        bit //= 2
-    return held.reshape((-1,) + value.shape[1:])
+    held = [value[None]]
+    for ahead in range(1, 4):
+        held.append(lax.ppermute(value[None], axis, [(source, (source - 4 * ahead) % count) for source in range(count)]))
+    held = jnp.concatenate(held, axis=0)
+    held = jnp.concatenate([held, lax.ppermute(held, axis, [(source, source ^ 2) for source in range(count)])], axis=0)
+    return held, lax.ppermute(held, axis, [(source, source ^ 1) for source in range(count)])
 
 
 def local_gathered(
@@ -452,21 +558,21 @@
     width = enc_weight.shape[1]
     count = lax.axis_size("tm")
     samples = waveform.reshape(-1, LANES)
-    gathered = gather_doubling(samples, "tm")
-    wave = jnp.concatenate([gathered, jnp.zeros((16, LANES), jnp.float32)], axis=0)
+    near, far = gather_chunks(samples, "tm")
     own_rows = samples.shape[0]
     place = lax.axis_index("tm").reshape(1)
     weights = (intra_qkv, intra_out, intra_up, intra_down, inter_qkv, inter_out, inter_up, inter_down)
-    act, own = core_call(place, wave, enc_weight, *weights, own_rows)
+    act, own = core_call(place, near, far, enc_weight, *weights)
     pieces = act.reshape(count, own_rows, width)
-    vmem = pl.BlockSpec(memory_space=pltpu.VMEM)
     received = lax.all_to_all(pieces, "tm", split_axis=0, concat_axis=0, tiled=True)
+    whole = pl.BlockSpec(own.shape, lambda speaker: (0, 0, 0))
     return pl.pallas_call(
         mask_kernel,
+        grid=(2,),
         out_shape=jax.ShapeDtypeStruct((2, 16 * own_rows, width), jnp.bfloat16),
-        in_specs=[vmem] * 3,
-        out_specs=vmem,
-        scratch_shapes=[pltpu.VMEM((2, width // LANES, 16 * own_rows, LANES), jnp.float32)],
+        in_specs=[whole, whole, pl.BlockSpec((width, width), lambda speaker: (0, speaker))],
+        out_specs=pl.BlockSpec((1, 16 * own_rows, width), lambda speaker: (speaker, 0, 0)),
+        scratch_shapes=[pltpu.VMEM((width // LANES, 16 * own_rows, LANES), jnp.float32)],
         compiler_params=pltpu.CompilerParams(vmem_limit_bytes=32 * 1024 * 1024),
         name="mask",
     )(received, own, mask_weight)

time: 106 us -> 87.4 us (0.82)
  Pallas kernels: 67 us -> 49.9 us
  waiting for transfers between devices: 10.1 us -> 6.92 us
  starting transfers between devices: 7.43 us -> 8.65 us
    pallas_call x1, Pallas kernels: 64.4 us -> 47.7 us  [core_call(): pl.pallas_call(core_kernel, out_shape=(jax.ShapeDtypeStruct((rows_total,...]
    ppermute x4 -> x5, waiting for transfers between devices: 10.1 us -> 6.92 us  [the longest x1 3.42 us: gather_chunks(): lax.ppermute(held, axis, [(source, source ^ 2) for source in range(count)])]
    unnamed x6 -> x14, local copies, waits for them, and re-layouts: 0.01 us -> 1.52 us
    ppermute x4 -> x5, starting transfers between devices: 7.43 us -> 8.65 us  [the longest x3 6.99 us: gather_chunks(): lax.ppermute(value[None], axis, [(source, (source - 4 * ahead) % count) f...]
  transfers between devices with their start and end apart: 4 -> 5, of which waited for: 4 -> 4; matrix products, arithmetic and copies ran while one was open for 0% -> 1% of each run, Pallas kernels for 0% -> 0%
where the time goes in v2:
time: 87.4 us; the launch traced here: 87 us
  Pallas kernels  49.9 us (57%)
  blocking collectives  19.9 us (23%)
  starting transfers between devices  8.65 us (10%)
  waiting for transfers between devices  6.92 us (8%)
  local copies, waits for them, and re-layouts  1.53 us (2%)
    pallas_call x1, Pallas kernels, core_call(): pl.pallas_call(core_kernel, out_shape=(jax.ShapeDtypeStruct((rows_total,...  47.7 us
    all_to_all x1, blocking collectives, local_gathered(): lax.all_to_all(pieces, 'tm', split_axis=0, concat_axis=0, tiled=True)  19.9 us
    ppermute x3, starting transfers between devices, gather_chunks(): lax.ppermute(value[None], axis, [(source, (source - 4 * ahead) % count) f...  6.99 us
    ppermute x1, waiting for transfers between devices, gather_chunks(): lax.ppermute(held, axis, [(source, source ^ 2) for source in range(count)])  3.42 us
    pallas_call x1, Pallas kernels, local_gathered(): pl.pallas_call(mask_kernel, grid=(2,), out_shape=jax.ShapeDtypeStruct((2,...  2.23 us
    ppermute x3, waiting for transfers between devices, gather_chunks(): lax.ppermute(value[None], axis, [(source, (source - 4 * ahead) % count) f...  1.98 us
  transfers between devices with their start and end apart: 5, of which 4 were waited for; matrix products, arithmetic and copies ran while one was open for 1% of the time, Pallas kernels for 0%

profile of v2, /device:TPU:0, one launch (start us, length us, event | category | flops | bytes accessed | tf_op | source)
XLA Modules:
  0.0 87.0 jit_solution(1162818449022386506)
XLA Ops:
  0.0 0.0 copy-start.4
  0.0 3.1 %collective-permute-start.2 = (f32[1,64,128]{2,1,0:T(8,128)}, f32[1,64,128]{2,1,0:T(8,128)S(1)}, u32[]{:S(2)}, u32[]{:S(2)}) collective-permute-start(f32[1,64,128]{2,1,0:T(8,128)} %bitcast.5), channel_id=1, source_target_pairs={{0,4},{1,5},{2,6},{3,7},{4,8},{5,9},{6,10},{7,11},{8,12},{9,13},{1... | collective-permute-start | bytes 98312 | tf_op jit(solution)/shard_map/ppermute | solution.py:539
  3.1 2.6 %collective-permute-start.1 = (f32[1,64,128]{2,1,0:T(8,128)}, f32[1,64,128]{2,1,0:T(8,128)S(1)}, u32[]{:S(2)}, u32[]{:S(2)}) collective-permute-start(f32[1,64,128]{2,1,0:T(8,128)} %bitcast.6), channel_id=1, source_target_pairs={{0,8},{1,9},{2,10},{3,11},{4,12},{5,13},{6,14},{7,15},{8,0},{9,1},... | collective-permute-start | bytes 98312 | tf_op jit(solution)/shard_map/ppermute | solution.py:539
  5.6 1.3 %collective-permute-start = (f32[1,64,128]{2,1,0:T(8,128)}, f32[1,64,128]{2,1,0:T(8,128)S(1)}, u32[]{:S(2)}, u32[]{:S(2)}) collective-permute-start(f32[1,64,128]{2,1,0:T(8,128)} %bitcast.7), channel_id=1, source_target_pairs={{0,12},{1,13},{2,14},{3,15},{4,0},{5,1},{6,2},{7,3},{8,4},{9,5},{1... | collective-permute-start | bytes 98312 | tf_op jit(solution)/shard_map/ppermute | solution.py:539
  7.0 0.8 constant_dynamic-update-slice_fusion.4
  7.8 0.0 collective-permute-done.2
  7.8 0.6 collective-permute-done.1
  8.4 1.3 %collective-permute-done = f32[1,64,128]{2,1,0:T(8,128)S(1)} collective-permute-done((f32[1,64,128]{2,1,0:T(8,128)}, f32[1,64,128]{2,1,0:T(8,128)S(1)}, u32[]{:S(2)}, u32[]{:S(2)}) %collective-permute-start) | collective-permute-done | bytes 32800 | tf_op jit(solution)/shard_map/ppermute | solution.py:539
  9.8 0.0 copy-done.4
  9.8 1.6 %collective-permute-start.3 = (f32[4,64,128]{2,1,0:T(8,128)S(1)}, f32[4,64,128]{2,1,0:T(8,128)S(1)}, u32[]{:S(2)}, u32[]{:S(2)}) collective-permute-start(f32[4,64,128]{2,1,0:T(8,128)S(1)} %pad_maximum_fusion), channel_id=1, source_target_pairs={{0,2},{1,3},{2,0},{3,1},{4,6},{5,7},{6,4},{7,5},{8,10},{9,11},{10,... | collective-permute-start | bytes 393224 | tf_op jit(solution)/shard_map/ppermute | solution.py:541
  11.4 3.4 %collective-permute-done.3 = f32[4,64,128]{2,1,0:T(8,128)S(1)} collective-permute-done((f32[4,64,128]{2,1,0:T(8,128)S(1)}, f32[4,64,128]{2,1,0:T(8,128)S(1)}, u32[]{:S(2)}, u32[]{:S(2)}) %collective-permute-start.3) | collective-permute-done | bytes 131104 | tf_op jit(solution)/shard_map/ppermute | solution.py:541
  14.8 0.0 copy-start.2
  14.8 0.1 collective-permute-start.4
  14.9 1.5 %collective-permute-done.4.far_ref = f32[8,64,128]{2,1,0:T(8,128)S(1)} collective-permute-done((f32[8,64,128]{2,1,0:T(8,128)S(1)}, f32[8,64,128]{2,1,0:T(8,128)S(1)}, u32[]{:S(2)}, u32[]{:S(2)}) %collective-permute-start.4) | collective-permute-done | bytes 262176 | tf_op jit(solution)/shard_map/ppermute | solution.py:542
  16.4 0.0 copy-start.3
  16.4 0.0 copy-done.2
  16.5 0.7 copy-done.3
  17.1 47.7 %core.1 = (bf16[1024,256]{1,0:T(8,128)(2,1)}, bf16[16,64,256]{2,1,0:T(8,128)(2,1)}) custom-call(s32[1]{0:T(128)} %bitcast.place_ref, f32[8,64,128]{2,1,0:T(8,128)} %copy-done.2, f32[8,64,128]{2,1,0:T(8,128)} %copy-done.3, f32[16,256]{1,0:T(8,128)} %enc_ref.1, bf16[256,768]{1,0:T(8,128)(2,1)} %rest_0_.1, bf16[256,256]{1,0:T(8,128)(2,1)} %rest_1_.1, ...), custom_call_target="tpu_custom_call" | custom-call | tf_op jit(solution)/shard_map/core/pallas_call | solution.py:499
  64.8 0.0 copy-start
  64.8 0.0 copy-start.1
  64.9 19.9 %all_to_all.5.act_ref = bf16[16,64,256]{2,1,0:T(8,128)(2,1)S(1)} all-to-all(bf16[16,64,256]{2,1,0:T(8,128)(2,1)} %bitcast.4), channel_id=1, replica_groups=mesh['grp'=2,'tm'=16] {'tm'}, dimensions={0} | all-to-all | bytes 1048576 | tf_op jit(solution)/shard_map/all_to_all | solution.py:567
  84.8 0.0 copy-done
  84.8 0.0 copy-done.1
  84.8 2.2 %mask.1 = bf16[2,1024,256]{2,1,0:T(8,128)(2,1)} custom-call(bf16[16,64,256]{2,1,0:T(8,128)(2,1)S(1)} %all_to_all.5.act_ref, bf16[16,64,256]{2,1,0:T(8,128)(2,1)S(1)} %copy-done, bf16[256,512]{1,0:T(8,128)(2,1)S(1)} %copy-done.1), custom_call_target="tpu_custom_call" | custom-call | tf_op jit(solution)/shard_map/mask/pallas_call | solution.py:569
  (5 shorter events, 0.0 us)
Async XLA Ops:
  0.0 9.8 %copy-start.4 = (f32[8192]{0:T(1024)S(1)}, f32[8192]{0:T(1024)}, u32[]{:S(2)}) copy-start(f32[8192]{0:T(1024)} %param.11) | copy-start | bytes 98308
  0.0 7.8 %collective-permute-start.2 = (f32[1,64,128]{2,1,0:T(8,128)}, f32[1,64,128]{2,1,0:T(8,128)S(1)}, u32[]{:S(2)}, u32[]{:S(2)}) collective-permute-start(f32[1,64,128]{2,1,0:T(8,128)} %bitcast.5), channel_id=1, source_target_pairs={{0,4},{1,5},{2,6},{3,7},{4,8},{5,9},{6,10},{7,11},{8,12},{9,13},{1... | collective-permute-start | bytes 98312 | tf_op jit(solution)/shard_map/ppermute | solution.py:539
  3.1 5.4 %collective-permute-start.1 = (f32[1,64,128]{2,1,0:T(8,128)}, f32[1,64,128]{2,1,0:T(8,128)S(1)}, u32[]{:S(2)}, u32[]{:S(2)}) collective-permute-start(f32[1,64,128]{2,1,0:T(8,128)} %bitcast.6), channel_id=1, source_target_pairs={{0,8},{1,9},{2,10},{3,11},{4,12},{5,13},{6,14},{7,15},{8,0},{9,1},... | collective-permute-start | bytes 98312 | tf_op jit(solution)/shard_map/ppermute | solution.py:539
  5.6 4.1 %collective-permute-start = (f32[1,64,128]{2,1,0:T(8,128)}, f32[1,64,128]{2,1,0:T(8,128)S(1)}, u32[]{:S(2)}, u32[]{:S(2)}) collective-permute-start(f32[1,64,128]{2,1,0:T(8,128)} %bitcast.7), channel_id=1, source_target_pairs={{0,12},{1,13},{2,14},{3,15},{4,0},{5,1},{6,2},{7,3},{8,4},{9,5},{1... | collective-permute-start | bytes 98312 | tf_op jit(solution)/shard_map/ppermute | solution.py:539
  9.8 5.0 %collective-permute-start.3 = (f32[4,64,128]{2,1,0:T(8,128)S(1)}, f32[4,64,128]{2,1,0:T(8,128)S(1)}, u32[]{:S(2)}, u32[]{:S(2)}) collective-permute-start(f32[4,64,128]{2,1,0:T(8,128)S(1)} %pad_maximum_fusion), channel_id=1, source_target_pairs={{0,2},{1,3},{2,0},{3,1},{4,6},{5,7},{6,4},{7,5},{8,10},{9,11},{10,... | collective-permute-start | bytes 393224 | tf_op jit(solution)/shard_map/ppermute | solution.py:541
  14.8 1.6 %copy-start.2 = (f32[8,64,128]{2,1,0:T(8,128)}, f32[8,64,128]{2,1,0:T(8,128)S(1)}, u32[]{:S(2)}) copy-start(f32[8,64,128]{2,1,0:T(8,128)S(1)} %constant_dynamic-update-slice_fusion.near_ref) | copy-start | bytes 786436
  14.8 1.6 %collective-permute-start.4 = (f32[8,64,128]{2,1,0:T(8,128)S(1)}, f32[8,64,128]{2,1,0:T(8,128)S(1)}, u32[]{:S(2)}, u32[]{:S(2)}) collective-permute-start(f32[8,64,128]{2,1,0:T(8,128)S(1)} %constant_dynamic-update-slice_fusion.near_ref), channel_id=1, source_target_pairs={{0,1},{1,0},{2,3},{3,2},{4,5},{5,4},{6,7},{7,6},{8,9},{9,8},{10,11... | collective-permute-start | bytes 786440 | tf_op jit(solution)/shard_map/ppermute | solution.py:542
  16.4 0.7 copy-start.3
  64.8 19.9 %copy-start = (bf16[16,64,256]{2,1,0:T(8,128)(2,1)S(1)}, bf16[16,64,256]{2,1,0:T(8,128)(2,1)}, u32[]{:S(2)}) copy-start(bf16[16,64,256]{2,1,0:T(8,128)(2,1)} %get-tuple-element.8.own_ref) | copy-start | bytes 1572868
  64.8 19.9 %copy-start.1 = (bf16[256,512]{1,0:T(8,128)(2,1)S(1)}, bf16[256,512]{1,0:T(8,128)(2,1)}, u32[]{:S(2)}) copy-start(bf16[256,512]{1,0:T(8,128)(2,1)} %weight_ref.1) | copy-start | bytes 786436
